TPU v7x, 32 devices: a whole 2x2x4 slice. The times are simulated.
32 devices in a mesh: runs: 2 (over y), ctx: 4 (over z), head: 4 (over x, core).
Axes of the slice: x: 2, y: 2, z: 4, core: 2. Of those that a mesh axis runs over, the one named last changes fastest.
Arguments:
- tokens: bfloat16 [4096, 2048], P(('runs', 'ctx', 'head')), parts along dimension 0, may hold values from -400 to 400
- in_gain: float32 [2048], replicated, may hold values from 0.1 to 1.9
- projections: bfloat16 [3, 2048, 2048], P(None, 'ctx', 'head'), may hold values from -0.125 to 0.125
- prior_state: float32 [32, 128, 128], P(('runs', 'head')), parts along dimension 0, may hold values from -256 to 256
- out_gain: float32 [2048], P('head'), may hold values from 0.1 to 1.9
Outputs:
- attended: bfloat16 [4096, 2048], P(('runs', 'ctx', 'head')), parts along dimension 0
There are 2 independent parts, one for each index of `runs`. A program takes and returns all parts, laid end to end along the dimension named above; an argument that names none is the same for every part. Nothing has to cross between parts.
All inputs are finite; a program needn't handle non-finite values.
Results may differ from a plain program's by a relative error of at most 0.0071.
Values may be sent and summed in bfloat16 or wider, within the bound.
A program may use at most 64 MiB of HBM per device.

v0:
```python
import jax
import jax.numpy as jnp
from jax import lax
from jax.sharding import PartitionSpec as P

BLOCK = 512


def prefix(part, axis, combine, identity):
    place = lax.axis_index(axis)
    gathered = lax.all_gather(part, axis)
    state = jnp.zeros_like(part) + jnp.asarray(identity, part.dtype)

    def one(step, state):
        return combine(state, lax.dynamic_index_in_dim(gathered, step, 0, False))

    return lax.fori_loop(0, place, one, state)


def rms_tokens(values_in, gain):
    wide = values_in.astype(jnp.float32)
    scale = lax.rsqrt(jnp.mean(wide * wide, axis=-1, keepdims=True) + 1e-06)
    return (wide * scale * gain).astype(jnp.bfloat16)


def combine_sum(earlier, later):
    return earlier + later


def on_device(tokens, in_gain, projections, prior_state, out_gain):
    normed = rms_tokens(tokens, in_gain)
    width_here = projections.shape[2]
    heads_here = prior_state.shape[0]
    head_dim = prior_state.shape[1]
    full_weights = lax.all_gather(projections, "ctx", axis=1, tiled=True)
    mapped = jnp.einsum(
        "td,jdc->jtc",
        lax.all_gather(normed, "head", axis=0, tiled=True),
        full_weights,
        preferred_element_type=jnp.float32,
    ).astype(jnp.bfloat16)
    span_rows = mapped.shape[1]
    blocks = span_rows // BLOCK
    shaped = mapped.reshape(3, blocks, BLOCK, heads_here, head_dim)
    queries = shaped[0]
    keys_all = shaped[1]
    values_all = shaped[2]
    block_states = jnp.einsum(
        "bkhd,bkhe->bhde", keys_all, values_all, preferred_element_type=jnp.float32
    )
    local_total = jnp.sum(block_states, axis=0)
    before = prefix(local_total, "ctx", combine_sum, jnp.zeros_like(local_total))
    entering = prior_state + before
    starts = entering[None] + jnp.cumsum(block_states, axis=0) - block_states
    position = jnp.arange(BLOCK, dtype=jnp.int32)
    causal = position[:, None] >= position[None, :]
    scores = jnp.einsum("bqhd,bkhd->bhqk", queries, keys_all, preferred_element_type=jnp.float32)
    scores = jnp.where(causal[None, None], scores, 0.0).astype(jnp.bfloat16)
    intra = jnp.einsum("bhqk,bkhd->bqhd", scores, values_all, preferred_element_type=jnp.float32)
    inter = jnp.einsum(
        "bqhd,bhde->bqhe", queries, starts.astype(jnp.bfloat16), preferred_element_type=jnp.float32
    )
    mixed = intra + inter
    scale = lax.rsqrt(jnp.mean(mixed * mixed, axis=-1, keepdims=True) + 1e-06)
    gains = out_gain.reshape(heads_here, head_dim)
    result = (mixed * scale * gains).astype(jnp.bfloat16).reshape(span_rows, width_here)
    return lax.all_to_all(result, "head", split_axis=0, concat_axis=1, tiled=True)


def solution(mesh):
    in_specs = (
        P(("runs", "ctx", "head"), None),
        P(),
        P(None, "ctx", "head"),
        P(("runs", "head"), None, None),
        P("head"),
    )
    out_specs = P(("runs", "ctx", "head"), None)
    return jax.shard_map(
        on_device, mesh=mesh, in_specs=in_specs, out_specs=out_specs, check_vma=False
    )
```

profile of v0, /device:TPU:0, one launch (start us, length us, event | category | flops | bytes accessed | tf_op | source)
XLA Modules:
  0.0 211.0 jit_solution(1581802129097191559)
XLA Ops:
  6.5 1.3 fusion.11
  7.9 2.0 fusion.13
  9.9 0.0 all-gather.5.cloned.1.call-update
  9.9 0.0 all-gather.7.cloned.1.call-start
  10.0 1.6 copy.11
  11.6 0.0 all-gather.7.cloned.1.call-update
  11.6 0.0 all-gather.9.cloned.1.call-start
  11.7 23.7 %all-gather.5.cloned.1.call-done = bf16[512,2048]{1,0:T(8,128)(2,1)} async-done(((bf16[128,2048]{1,0:T(8,128)(2,1)}), bf16[512,2048]{1,0:T(8,128)(2,1)}) %all-gather.5.cloned.1.call-update) | async-done | bytes 2097168 | tf_op jit(solution)/shard_map/all_gather | solution.py:38
  35.4 117.0 %all-gather.7.cloned.1.call-done = bf16[3,2048,512]{1,2,0:T(8,128)(2,1)} async-done(((bf16[3,512,512]{1,2,0:T(8,128)(2,1)}), bf16[3,2048,512]{1,2,0:T(8,128)(2,1)}) %all-gather.7.cloned.1.call-update) | async-done | bytes 6291472 | tf_op jit(solution)/shard_map/all_gather | solution.py:35
  152.3 6.9 %fusion.6 = bf16[3,512,512]{1,2,0:T(8,128)(2,1)S(1)} fusion(bf16[3,2048,512]{1,2,0:T(8,128)(2,1)} %all-gather.7.cloned.1.call-done, bf16[512,2048]{1,0:T(8,128)(2,1)} %all-gather.5.cloned.1.call-done), kind=kOutput, calls=%fused_computation.6 | convolution fusion | flops 3222011904 | bytes 9961472 | tf_op jit(solution)/shard_map/td,jdc->jtc/dot_general | solution.py:36
  159.2 0.1 fusion.18
  159.4 1.0 fusion.19
  160.4 0.0 all-gather.9.cloned.1.call-update
  160.4 0.1 iota_compare_fusion
  160.5 26.2 %all-gather.9.cloned.1.call-done = f32[16,128,128]{2,1,0:T(8,128)} async-done(((f32[4,128,128]{2,1,0:T(8,128)}), f32[16,128,128]{2,1,0:T(8,128)}) %all-gather.9.cloned.1.call-update) | async-done | bytes 1048592 | tf_op jit(solution)/shard_map/all_gather | solution.py:11
  186.7 0.9 copy-done
  187.6 0.1 copy-done.2
  187.7 1.3 fusion.15
  189.0 2.6 %multiply_reduce_fusion = (f32[512,4]{0,1:T(4,128)S(1)}, f32[1,512,4,128]{1,3,2,0:T(8,128)S(1)}) fusion(f32[4,128,512]{2,1,0:T(8,128)} %fusion.15, bf16[512,4,128]{0,2,1:T(8,128)(2,1)S(1)} %bitcast.38, bf16[512,4,128]{0,2,1:T(8,128)(2,1)S(1)} %bitcast.42, bf16[512,4,128]{0,2,1:T(8,128)(2,1)S(1)} %bitcast.40, pred[512,512]{1,0:T(8,128)(4,1)S(1)} %iota_compare_fusion), kind=kOutput, calls=%fused_computation.15 | convolution fusion | flops 539752448 | bytes 3940352 | tf_op jit(solution)/shard_map/bhqk,bkhd->bqhd/dot_general | solution.py:59
  191.7 0.2 multiply_convert_fusion
  191.9 0.1 all_to_all.14
  192.0 0.1 copy.15
  192.1 11.4 %all_to_all.19 = bf16[4,128,512]{1,2,0:T(8,128)(2,1)S(1)} all-to-all(bf16[4,128,512]{1,2,0:T(8,128)(2,1)S(1)} %copy.15), channel_id=1, replica_groups=mesh['runs'=2,'ctx'=4,'head'=4] {'head'}, dimensions={0} | all-to-all | bytes 1048576 | tf_op jit(solution)/shard_map/all_to_all | solution.py:67
  203.5 1.0 copy.16
  (11 shorter events, 0.1 us)
Async XLA Ops:
  6.5 3.5 %copy-start.1 = (bf16[3,512,512]{2,1,0:T(8,128)(2,1)S(1)}, bf16[3,512,512]{2,1,0:T(8,128)(2,1)}, u32[]{:S(2)}) copy-start(bf16[3,512,512]{2,1,0:T(8,128)(2,1)} %param.9) | copy-start | bytes 4718596
  6.5 28.9 %all-gather.5.cloned.1.call-start = ((), (), s32[]{:S(2)}) async-start(), calls=%async_computation.1 | async-start | bytes 2621440 | tf_op jit(solution)/shard_map/all_gather | solution.py:38
  9.9 142.4 %all-gather.7.cloned.1.call-start = ((), (), s32[]{:S(2)}) async-start(), calls=%async_computation.2 | async-start | bytes 7864320 | tf_op jit(solution)/shard_map/all_gather | solution.py:35
  11.6 175.0 %all-gather.9.cloned.1.call-start = ((), (), s32[]{:S(2)}) async-start(), calls=%async_computation.3 | async-start | bytes 1310720 | tf_op jit(solution)/shard_map/all_gather | solution.py:11
  186.7 1.0 copy-start
  186.7 1.0 copy-start.2
  189.0 2.7 %copy-start.3 = (f32[512]{0:T(512)S(1)}, f32[512]{0:T(512)}, u32[]{:S(2)}) copy-start(f32[512]{0:T(512)} %param.11) | copy-start | bytes 6148
Sparse Core Ops, SparseCore 0:
  10.1 25.2 all-gather.4
  37.0 115.3 all-gather.6
  160.5 26.1 all-gather.8
where the time goes:
time: 211 us
  waiting for transfers between devices  167 us (79%)
  between operations  13.2 us (6%)
  matrix products  11.9 us (6%)
  blocking collectives  11.4 us (5%)
  local copies, waits for them, and re-layouts  3.93 us (2%)
  other arithmetic  3.62 us (2%)
    all_gather x1, waiting for transfers between devices, on_device(): full_weights = lax.all_gather(projections, 'ctx', axis=1, tiled=True)  117 us
    all_gather x1, waiting for transfers between devices, prefix(): gathered = lax.all_gather(part, axis)  26.2 us
    all_gather x1, waiting for transfers between devices, on_device(): lax.all_gather(normed, 'head', axis=0, tiled=True)  23.7 us
    all_to_all x1, blocking collectives, on_device(): lax.all_to_all(result, 'head', split_axis=0, concat_axis=1, tiled=True)  11.4 us
    dot_general x1, matrix products, on_device(): jnp.einsum('td,jdc->jtc', lax.all_gather(normed, 'head', axis=0, tiled=Tr...  6.89 us
  transfers between devices with their start and end apart: 3, of which 3 were waited for; matrix products, arithmetic and copies ran while one was open for 1% of the time, Pallas kernels for 0%

commit v1 on v0

v1 whole, which is shorter than its diff:
```python
import functools

import jax
import jax.numpy as jnp
from jax import lax
from jax.experimental import pallas as pl
from jax.experimental.pallas import tpu as pltpu
from jax.sharding import PartitionSpec as P

BLOCK = 512
CORES = 2
MESH = pl.DeviceIdType.MESH
QUERY, KEY, VALUE = 0, 1, 2


def dot(a, b, contract=((1,), (0,))):
    return lax.dot_general(a, b, (contract, ((), ())), preferred_element_type=jnp.float32)


def kernel(
    n_ctx, n_head,
    tok_ref, gain_ref, w_ref, prior_ref, og_ref,
    out_ref,
    x_buf, w_buf, q_buf, k_buf, v_buf, att, sums, totals, others, starts,
    own_sem, tz_send, tz_recv, tx_send, tx_recv, tc_send, tc_recv,
    wz_send, wz_recv, wy_send, wy_recv, st_send, st_recv, o_send, o_recv, o_own,
):
    run = lax.axis_index("runs")
    z = lax.axis_index("ctx")
    h = lax.axis_index("head")
    n_x = n_head // CORES
    x, core = h // CORES, h % CORES
    half = z % 2
    partner = z + 1 - 2 * half
    rows_here = tok_ref.shape[0]
    rows = w_ref.shape[1]
    rows_half = rows // 2
    heads_here = prior_ref.shape[0]
    mine = heads_here // 2
    dim = prior_ref.shape[1]
    width = mine * dim
    n_tok = x_buf.shape[0]
    span = n_tok // 2
    n_blocks = n_tok // BLOCK
    n_pairs = n_ctx // 2
    other_run = {"runs": 1 - run}

    def slot(side, head):
        return pl.ds(pl.multiple_of((side * n_head + head) * rows_here, rows_here), rows_here)

    def cols(side):
        return pl.ds(pl.multiple_of(side * width, width), width)

    def w_rows(source, part):
        start = pl.multiple_of(source * rows + part * rows_half, rows_half)
        return pl.ds(start, rows_half)

    own_w = pltpu.make_async_copy(
        w_ref.at[:, :, cols(half)],
        w_buf.at[:, pl.ds(pl.multiple_of(z * rows, rows), rows), :],
        own_sem,
    )
    own_w.start()

    barrier = pltpu.get_barrier_semaphore()
    greeted = [other_run]
    greeted += [{"ctx": (z + k) % n_ctx} for k in range(1, n_ctx)]
    greeted += [{"head": (h + k) % n_head} for k in range(1, n_head)]
    greeted += [{"ctx": partner, "head": (h + k) % n_head} for k in range(1, n_head)]
    for device in greeted:
        pl.semaphore_signal(barrier, inc=1, device_id=device, device_id_type=MESH)

    wide = tok_ref[...].astype(jnp.float32)
    scale = lax.rsqrt(jnp.mean(wide * wide, axis=-1, keepdims=True) + 1e-06)
    x_buf[slot(half, h), :] = (wide * scale * gain_ref[...]).astype(jnp.bfloat16)
    pl.semaphore_wait(barrier, len(greeted))

    sent = []

    def send(src, dst, send_sem, recv_sem, device):
        copy = pltpu.make_async_remote_copy(
            src_ref=src, dst_ref=dst, send_sem=send_sem, recv_sem=recv_sem,
            device_id=device, device_id_type=MESH,
        )
        copy.start()
        sent.append(copy)

    def arrived(dst, send_sem, recv_sem):
        pltpu.make_async_remote_copy(
            src_ref=dst, dst_ref=dst, send_sem=send_sem, recv_sem=recv_sem,
            device_id=other_run, device_id_type=MESH,
        ).wait_recv()

    def spread(side, b):
        block = x_buf.at[slot(side, h), :]
        for d in range(1, n_x):
            send(block, block, tx_send.at[d, b], tx_recv.at[d, b],
                 {"head": ((x + d) % n_x) * CORES + core})
        send(block, block, tc_send.at[0, b], tc_recv.at[0, b],
             {"head": x * CORES + 1 - core})

    def pass_on(side, b):
        for d in range(1, n_x):
            head = ((x + n_x - d) % n_x) * CORES + core
            block = x_buf.at[slot(side, head), :]
            arrived(block, tx_send.at[d, b], tx_recv.at[d, b])
            send(block, block, tc_send.at[d, b], tc_recv.at[d, b],
                 {"head": x * CORES + 1 - core})

    def send_weights(j):
        for k in range(1, n_ctx):
            to = (z + k) % n_ctx
            part = pl.ds(pl.multiple_of(run * rows_half, rows_half), rows_half)
            send(w_ref.at[j, part, cols(to % 2)], w_buf.at[j, w_rows(z, run), :],
                 wz_send.at[j, k], wz_recv.at[j, k], {"ctx": to})

    def swap_weights(j):
        for k in range(1, n_ctx):
            piece = w_buf.at[j, w_rows((z + n_ctx - k) % n_ctx, run), :]
            arrived(piece, wz_send.at[j, k], wz_recv.at[j, k])
            send(piece, piece, wy_send.at[j, k], wy_recv.at[j, k], other_run)

    def wait_weights(j):
        for k in range(1, n_ctx):
            piece = w_buf.at[j, w_rows((z + n_ctx - k) % n_ctx, 1 - run), :]
            arrived(piece, wy_send.at[j, k], wy_recv.at[j, k])

    def project(j, to):
        def tile(step, carry):
            at = pl.ds(pl.multiple_of(step * 256, 256), 256)
            to[at, :] = dot(x_buf[at, :], w_buf[j]).astype(jnp.bfloat16)
            return carry

        lax.fori_loop(0, n_tok // 256, tile, 0)

    block = x_buf.at[slot(half, h), :]
    send(block, block, tz_send, tz_recv, {"ctx": partner})
    spread(half, 0)
    send_weights(KEY)
    send_weights(VALUE)
    send_weights(QUERY)
    arrived(x_buf.at[slot(1 - half, h), :], tz_send, tz_recv)
    spread(1 - half, 1)
    pass_on(half, 0)
    swap_weights(KEY)
    pass_on(1 - half, 1)
    swap_weights(VALUE)
    for d in range(n_x):
        head = ((x + n_x - d) % n_x) * CORES + 1 - core
        for b, side in ((0, half), (1, 1 - half)):
            arrived(x_buf.at[slot(side, head), :], tc_send.at[d, b], tc_recv.at[d, b])
    own_w.wait()
    wait_weights(KEY)
    project(KEY, k_buf)
    swap_weights(QUERY)
    wait_weights(VALUE)
    project(VALUE, v_buf)

    for i in range(mine):
        at = pl.ds(i * dim, dim)
        total = None
        for b in range(n_blocks):
            here = pl.ds(b * BLOCK, BLOCK)
            one = dot(k_buf[here, at], v_buf[here, at], ((0,), (0,)))
            sums[b, i] = one
            total = one if total is None else total + one
        totals[i] = total
    for k in range(1, n_pairs):
        send(totals, others.at[k], st_send.at[k], st_recv.at[k], {"ctx": (z + 2 * k) % n_ctx})

    wait_weights(QUERY)
    project(QUERY, q_buf)

    for k in range(1, n_pairs):
        arrived(others.at[k], st_send.at[k], st_recv.at[k])
    for i in range(mine):
        state = prior_ref[half * mine + i]
        for k in range(1, n_pairs):
            state = state + jnp.where(z >= 2 * k, others[k, i], 0.0)
        for b in range(n_blocks):
            starts[b, i] = state.astype(jnp.bfloat16)
            state = state + sums[b, i]

    step_rows = 256
    out_cols = pl.ds(pl.multiple_of((h * 2 + half) * width, width), width)
    per_span = span // BLOCK
    for dz in (1, 0):
        side = (half + dz) % 2
        for bb in range(per_span):
            b = side * per_span + bb
            base = pl.multiple_of(b * BLOCK, BLOCK)
            for i in range(mine):
                at = pl.ds(i * dim, dim)
                gains = og_ref[half * mine + i]
                start = starts[b, i]
                for r in range(0, BLOCK, step_rows):
                    seen = r + step_rows
                    here = pl.ds(pl.multiple_of(base + r, step_rows), step_rows)
                    query = q_buf[here, at]
                    before = pl.ds(base, seen)
                    scores = dot(query, k_buf[before, at], ((1,), (1,)))
                    row = lax.broadcasted_iota(jnp.int32, (step_rows, seen), 0) + r
                    col = lax.broadcasted_iota(jnp.int32, (step_rows, seen), 1)
                    scores = jnp.where(row >= col, scores, 0.0).astype(jnp.bfloat16)
                    mixed = dot(scores, v_buf[before, at]) + dot(query, start)
                    level = lax.rsqrt(jnp.mean(mixed * mixed, axis=-1, keepdims=True) + 1e-06)
                    att[here, at] = (mixed * level * gains).astype(jnp.bfloat16)
        for dh in range(n_head):
            if dz == 0 and dh == 0:
                continue
            head = (h + dh) % n_head
            send(att.at[slot(side, head), :], out_ref.at[:, out_cols],
                 o_send.at[dz, dh], o_recv.at[dz, dh],
                 {"ctx": z + side - half, "head": head})
    own_out = pltpu.make_async_copy(att.at[slot(half, h), :], out_ref.at[:, out_cols], o_own)
    own_out.start()
    own_out.wait()
    for dz in (1, 0):
        for dh in range(n_head):
            if dz == 0 and dh == 0:
                continue
            source = ((h + n_head - dh) % n_head) * 2 + (half + dz) % 2
            place = pl.ds(pl.multiple_of(source * width, width), width)
            arrived(out_ref.at[:, place], o_send.at[dz, dh], o_recv.at[dz, dh])
    for copy in sent:
        copy.wait_send()


def on_device(n_ctx, n_head, tokens, in_gain, projections, prior_state, out_gain):
    rows_here, features = tokens.shape
    heads_here, dim, _ = prior_state.shape
    mine = heads_here // 2
    width = mine * dim
    n_tok = 2 * n_head * rows_here
    n_blocks = n_tok // BLOCK
    n_x = n_head // CORES
    dma = pltpu.SemaphoreType.DMA
    vmem = pl.BlockSpec(memory_space=pltpu.VMEM)
    bf16, f32 = jnp.bfloat16, jnp.float32
    return pl.pallas_call(
        functools.partial(kernel, n_ctx, n_head),
        out_shape=jax.ShapeDtypeStruct((rows_here, features), bf16),
        in_specs=[vmem, vmem, pl.BlockSpec(memory_space=pl.ANY), vmem, vmem],
        out_specs=vmem,
        scratch_shapes=[
            pltpu.VMEM((n_tok, features), bf16),
            pltpu.VMEM((3, features, width), bf16),
            pltpu.VMEM((n_tok, width), bf16),
            pltpu.VMEM((n_tok, width), bf16),
            pltpu.VMEM((n_tok, width), bf16),
            pltpu.VMEM((n_tok, width), bf16),
            pltpu.VMEM((n_blocks, mine, dim, dim), f32),
            pltpu.VMEM((mine, dim, dim), f32),
            pltpu.VMEM((n_ctx // 2, mine, dim, dim), f32),
            pltpu.VMEM((n_blocks, mine, dim, dim), bf16),
            dma, dma, dma,
            dma((n_x, 2)), dma((n_x, 2)), dma((n_x, 2)), dma((n_x, 2)),
            dma((3, n_ctx)), dma((3, n_ctx)), dma((3, n_ctx)), dma((3, n_ctx)),
            dma((n_ctx // 2,)), dma((n_ctx // 2,)),
            dma((2, n_head)), dma((2, n_head)), dma,
        ],
        compiler_params=pltpu.CompilerParams(
            collective_id=0, has_side_effects=True, vmem_limit_bytes=50 * 1024 * 1024
        ),
    )(
        tokens,
        in_gain.reshape(1, features),
        projections,
        prior_state,
        out_gain.reshape(heads_here, 1, dim),
    )


def solution(mesh):
    in_specs = (
        P(("runs", "ctx", "head"), None),
        P(),
        P(None, "ctx", "head"),
        P(("runs", "head"), None, None),
        P("head"),
    )
    out_specs = P(("runs", "ctx", "head"), None)
    return jax.shard_map(
        functools.partial(on_device, mesh.shape["ctx"], mesh.shape["head"]),
        mesh=mesh, in_specs=in_specs, out_specs=out_specs, check_vma=False,
    )
```

time: 211 us -> 74.6 us (0.35)
  waiting for transfers between devices: 167 us -> 0 us
  Pallas kernels: 0 us -> 68.8 us
  between operations: 13.2 us -> 0.01 us
  matrix products: 11.9 us -> 0 us
  blocking collectives: 11.4 us -> 0 us
  other arithmetic: 3.62 us -> 0 us
    all_gather x3 -> x0, waiting for transfers between devices: 167 us -> none  [the longest x1 117 us: on_device(): full_weights = lax.all_gather(projections, 'ctx', axis=1, tiled=True)]
    pallas_call x0 -> x1, Pallas kernels: none -> 68.8 us  [on_device(): pl.pallas_call(functools.partial(kernel, n_ctx, n_head), out_shape=jax.Sh...]
    dot_general x4 -> x0, matrix products: 11.9 us -> none  [the longest x1 6.89 us: on_device(): jnp.einsum('td,jdc->jtc', lax.all_gather(normed, 'head', axis=0, tiled=Tr...]
    all_to_all x1 -> x0, blocking collectives: 11.4 us -> none  [on_device(): lax.all_to_all(result, 'head', split_axis=0, concat_axis=1, tiled=True)]
    unnamed x9 -> x11, local copies, waits for them, and re-layouts: 2.6 us -> 5.57 us
    convert_element_type x2 -> x0, other arithmetic: 2.18 us -> none  [the longest x1 2.03 us: rms_tokens(): return (wide * scale * gain).astype(jnp.bfloat16)]
  transfers between devices with their start and end apart: 3 -> 0, of which waited for: 3 -> 0; matrix products, arithmetic and copies ran while one was open for 1% -> 0% of each run, Pallas kernels for 0% -> 0%
where the time goes in v1:
time: 74.6 us; the launch traced here: 74.4 us
  Pallas kernels  68.8 us (92%)
  local copies, waits for them, and re-layouts  5.57 us (7%)
    pallas_call x1, Pallas kernels, on_device(): pl.pallas_call(functools.partial(kernel, n_ctx, n_head), out_shape=jax.Sh...  68.8 us
    unnamed x11, local copies, waits for them, and re-layouts  5.57 us

profile of v1, /device:TPU:0, one launch (start us, length us, event | category | flops | bytes accessed | tf_op | source)
XLA Modules:
  0.0 74.4 jit_solution(298127283057333699)
XLA Ops:
  0.0 0.0 copy-start
  0.0 1.4 %copy-done = bf16[3,512,512]{2,1,0:T(8,128)(2,1)S(1)} copy-done((bf16[3,512,512]{2,1,0:T(8,128)(2,1)S(1)}, bf16[3,512,512]{2,1,0:T(8,128)(2,1)}, u32[]{:S(2)}) %copy-start) | copy-done | bytes 1572888
  1.4 0.0 copy-start.1
  1.4 1.0 %copy-done.1 = bf16[128,2048]{1,0:T(8,128)(2,1)S(1)} copy-done((bf16[128,2048]{1,0:T(8,128)(2,1)S(1)}, bf16[128,2048]{1,0:T(8,128)(2,1)}, u32[]{:S(2)}) %copy-start.1) | copy-done | bytes 524312
  2.5 0.0 copy-start.2
  2.5 0.9 %copy-done.2 = f32[4,128,128]{2,1,0:T(8,128)S(1)} copy-done((f32[4,128,128]{2,1,0:T(8,128)S(1)}, f32[4,128,128]{2,1,0:T(8,128)}, u32[]{:S(2)}) %copy-start.2) | copy-done | bytes 262168
  3.4 0.0 copy-start.3
  3.4 0.7 copy-done.3
  4.1 0.0 copy-start.4
  4.1 0.7 copy-done.4
  4.8 68.8 %shard_map.55 = bf16[128,2048]{1,0:T(8,128)(2,1)S(1)} custom-call(bf16[128,2048]{1,0:T(8,128)(2,1)S(1)} %copy-done.1, f32[1,2048]{1,0:T(1,128)S(1)} %bitcast.2, bf16[3,512,512]{2,1,0:T(8,128)(2,1)S(1)} %copy-done, f32[4,128,128]{2,1,0:T(8,128)S(1)} %copy-done.2, f32[4,1,128]{2,1,0:T(1,128)S(1)} %bitcast.3), custom_call_target="tpu_custom_call" | custom-call | tf_op jit(solution)/shard_map/pallas_call | solution.py:240
  73.6 0.8 %copy.7 = bf16[128,2048]{1,0:T(8,128)(2,1)} copy(bf16[128,2048]{1,0:T(8,128)(2,1)S(1)} %shard_map.55) | data formatting | bytes 1048576
Async XLA Ops:
  0.0 1.4 %copy-start = (bf16[3,512,512]{2,1,0:T(8,128)(2,1)S(1)}, bf16[3,512,512]{2,1,0:T(8,128)(2,1)}, u32[]{:S(2)}) copy-start(bf16[3,512,512]{2,1,0:T(8,128)(2,1)} %w_ref.1) | copy-start | bytes 4718596
  1.4 1.0 %copy-start.1 = (bf16[128,2048]{1,0:T(8,128)(2,1)S(1)}, bf16[128,2048]{1,0:T(8,128)(2,1)}, u32[]{:S(2)}) copy-start(bf16[128,2048]{1,0:T(8,128)(2,1)} %tok_ref.1) | copy-start | bytes 1572868
  2.5 0.9 %copy-start.2 = (f32[4,128,128]{2,1,0:T(8,128)S(1)}, f32[4,128,128]{2,1,0:T(8,128)}, u32[]{:S(2)}) copy-start(f32[4,128,128]{2,1,0:T(8,128)} %prior_ref.1) | copy-start | bytes 786436
  3.4 0.7 copy-start.3
  4.1 0.7 copy-start.4

commit v2 on v1

v2 whole, which is shorter than its diff:
```python
import functools

import jax
import jax.numpy as jnp
from jax import lax
from jax.experimental import pallas as pl
from jax.experimental.pallas import tpu as pltpu
from jax.sharding import PartitionSpec as P

BLOCK = 512
CORES = 2
MESH = pl.DeviceIdType.MESH
QUERY, KEY, VALUE = 0, 1, 2
AHEAD = 6
AT_PARTNER, AT_FIRST, AT_SECOND, AT_KEYS, AT_VALUES = 2, 3, 7, 11, 12


def dot(a, b, contract=((1,), (0,))):
    return lax.dot_general(a, b, (contract, ((), ())), preferred_element_type=jnp.float32)


def kernel(
    n_ctx, n_head,
    tok_hbm, gain_hbm, w_ref, prior_hbm, og_hbm,
    out_ref,
    tok_ref, gain_ref, prior_ref, og_ref, in_sems,
    x_buf, w_buf, q_buf, k_buf, v_buf, att, sums, totals, others, starts,
    own_sem, tz_send, tz_recv, tx_send, tx_recv, tc_send, tc_recv,
    wz_send, wz_recv, wy_send, wy_recv, st_send, st_recv, oz_send, oz_recv, o_send, o_recv, o_own,
):
    run = lax.axis_index("runs")
    z = lax.axis_index("ctx")
    h = lax.axis_index("head")
    n_x = n_head // CORES
    x, core = h // CORES, h % CORES
    half = z % 2
    partner = z + 1 - 2 * half
    rows_here = tok_ref.shape[0]
    rows = w_ref.shape[1]
    rows_half = rows // 2
    cuts = wz_send.shape[0] // 3
    rows_cut = rows_half // cuts
    stages = [(j, cut) for j in (KEY, VALUE, QUERY) for cut in range(cuts)]
    mine = prior_ref.shape[0]
    dim = prior_ref.shape[1]
    width = mine * dim
    n_tok = x_buf.shape[0]
    span = n_tok // 2
    n_blocks = n_tok // BLOCK
    n_pairs = n_ctx // 2
    other_run = {"runs": 1 - run}

    def slot(side, head):
        return pl.ds(pl.multiple_of((side * n_head + head) * rows_here, rows_here), rows_here)

    def cols(side):
        return pl.ds(pl.multiple_of(side * width, width), width)

    def w_rows(source, part, cut):
        start = pl.multiple_of(source * rows + part * rows_half + cut * rows_cut, rows_cut)
        return pl.ds(start, rows_cut)

    own_w = pltpu.make_async_copy(
        w_ref.at[:, :, cols(half)],
        w_buf.at[:, pl.ds(pl.multiple_of(z * rows, rows), rows), :],
        own_sem,
    )
    my_heads = pl.ds(half * mine, mine)
    loads = [
        pltpu.make_async_copy(src, dst, in_sems.at[n])
        for n, (src, dst) in enumerate((
            (tok_hbm, tok_ref), (gain_hbm, gain_ref),
            (prior_hbm.at[my_heads], prior_ref), (og_hbm.at[my_heads], og_ref),
        ))
    ]
    for load in loads:
        load.start()
    own_w.start()

    barrier = pltpu.get_barrier_semaphore()
    greeted = [other_run]
    greeted += [{"ctx": (z + k) % n_ctx} for k in range(1, n_ctx)]
    greeted += [{"head": (h + k) % n_head} for k in range(1, n_head)]
    greeted += [{"ctx": partner, "head": (h + k) % n_head} for k in range(1, n_head)]
    for device in greeted:
        pl.semaphore_signal(barrier, inc=1, device_id=device, device_id_type=MESH)

    loads[0].wait()
    loads[1].wait()
    wide = tok_ref[...].astype(jnp.float32)
    scale = lax.rsqrt(jnp.mean(wide * wide, axis=-1, keepdims=True) + 1e-06)
    x_buf[slot(half, h), :] = (wide * scale * gain_ref[...]).astype(jnp.bfloat16)
    pl.semaphore_wait(barrier, len(greeted))

    sent = []

    def send(src, dst, send_sem, recv_sem, device):
        copy = pltpu.make_async_remote_copy(
            src_ref=src, dst_ref=dst, send_sem=send_sem, recv_sem=recv_sem,
            device_id=device, device_id_type=MESH,
        )
        copy.start()
        sent.append(copy)

    def arrived(dst, send_sem, recv_sem):
        pltpu.make_async_remote_copy(
            src_ref=dst, dst_ref=dst, send_sem=send_sem, recv_sem=recv_sem,
            device_id=other_run, device_id_type=MESH,
        ).wait_recv()

    def spread(side, b):
        block = x_buf.at[slot(side, h), :]
        for d in range(1, n_x):
            send(block, block, tx_send.at[d, b], tx_recv.at[d, b],
                 {"head": ((x + d) % n_x) * CORES + core})
        send(block, block, tc_send.at[0, b], tc_recv.at[0, b],
             {"head": x * CORES + 1 - core})

    def pass_on(side, b):
        for d in range(1, n_x):
            head = ((x + n_x - d) % n_x) * CORES + core
            block = x_buf.at[slot(side, head), :]
            arrived(block, tx_send.at[d, b], tx_recv.at[d, b])
            send(block, block, tc_send.at[d, b], tc_recv.at[d, b],
                 {"head": x * CORES + 1 - core})

    def send_weights(stage):
        j, cut = stages[stage]
        for k in range(1, n_ctx):
            to = (z + k) % n_ctx
            start = pl.multiple_of(run * rows_half + cut * rows_cut, rows_cut)
            send(w_ref.at[j, pl.ds(start, rows_cut), cols(to % 2)],
                 w_buf.at[j, w_rows(z, run, cut), :],
                 wz_send.at[stage, k], wz_recv.at[stage, k], {"ctx": to})

    def swap_weights(stage):
        j, cut = stages[stage]
        for k in range(1, n_ctx):
            piece = w_buf.at[j, w_rows((z + n_ctx - k) % n_ctx, run, cut), :]
            arrived(piece, wz_send.at[stage, k], wz_recv.at[stage, k])
            send(piece, piece, wy_send.at[stage, k], wy_recv.at[stage, k], other_run)

    def wait_weights(matrix):
        for stage, (j, cut) in enumerate(stages):
            if j != matrix:
                continue
            for k in range(1, n_ctx):
                piece = w_buf.at[j, w_rows((z + n_ctx - k) % n_ctx, 1 - run, cut), :]
                arrived(piece, wy_send.at[stage, k], wy_recv.at[stage, k])

    def project(j, to):
        def tile(step, carry):
            at = pl.ds(pl.multiple_of(step * 256, 256), 256)
            to[at, :] = dot(x_buf[at, :], w_buf[j]).astype(jnp.bfloat16)
            return carry

        lax.fori_loop(0, n_tok // 256, tile, 0)

    def start_tokens():
        block = x_buf.at[slot(half, h), :]
        send(block, block, tz_send, tz_recv, {"ctx": partner})
        spread(half, 0)

    def partner_tokens():
        arrived(x_buf.at[slot(1 - half, h), :], tz_send, tz_recv)
        spread(1 - half, 1)

    def wait_tokens():
        for d in range(n_x):
            head = ((x + n_x - d) % n_x) * CORES + 1 - core
            for b, side in ((0, half), (1, 1 - half)):
                arrived(x_buf.at[slot(side, head), :], tc_send.at[d, b], tc_recv.at[d, b])

    def do_keys():
        wait_weights(KEY)
        project(KEY, k_buf)

    def do_values():
        wait_weights(VALUE)
        project(VALUE, v_buf)

    def do_sums():
        for i in range(mine):
            at = pl.ds(i * dim, dim)
            total = None
            for b in range(n_blocks):
                here = pl.ds(b * BLOCK, BLOCK)
                one = dot(k_buf[here, at], v_buf[here, at], ((0,), (0,)))
                sums[b, i] = one
                total = one if total is None else total + one
            totals[i] = total
        for k in range(1, n_pairs):
            send(totals, others.at[k], st_send.at[k], st_recv.at[k],
                 {"ctx": (z + 2 * k) % n_ctx})

    def do_starts():
        for k in range(1, n_pairs):
            arrived(others.at[k], st_send.at[k], st_recv.at[k])
        for i in range(mine):
            state = prior_ref[i]
            for k in range(1, n_pairs):
                state = state + jnp.where(z >= 2 * k, others[k, i], 0.0)
            for b in range(n_blocks):
                starts[b, i] = state.astype(jnp.bfloat16)
                state = state + sums[b, i]

    n_stages = len(stages)
    ahead = min(AHEAD * cuts // 4, n_stages)
    between = [[] for _ in range(n_stages + 1)]
    for at, work in (
        (AT_PARTNER, (partner_tokens,)),
        (AT_FIRST, (functools.partial(pass_on, half, 0),)),
        (AT_SECOND, (functools.partial(pass_on, 1 - half, 1),)),
        (AT_KEYS, (wait_tokens, own_w.wait, loads[2].wait, loads[3].wait, do_keys)),
        (AT_VALUES, (do_values, do_sums)),
    ):
        between[at * cuts // 4] += work
    start_tokens()
    for stage in range(ahead):
        send_weights(stage)
    for stage in range(n_stages):
        for work in between[stage]:
            work()
        swap_weights(stage)
        if stage + ahead < n_stages:
            send_weights(stage + ahead)
    for work in between[n_stages]:
        work()
    do_starts()
    wait_weights(QUERY)
    project(QUERY, q_buf)

    step_rows = 256
    out_cols = pl.ds(pl.multiple_of((h * 2 + half) * width, width), width)
    per_span = span // BLOCK

    def attend(side, bb, r):
        b = side * per_span + bb
        base = pl.multiple_of(b * BLOCK, BLOCK)
        seen = r + step_rows
        here = pl.ds(pl.multiple_of(base + r, step_rows), step_rows)
        before = pl.ds(base, seen)
        row = lax.broadcasted_iota(jnp.int32, (step_rows, seen), 0) + r
        col = lax.broadcasted_iota(jnp.int32, (step_rows, seen), 1)
        for i in range(mine):
            at = pl.ds(i * dim, dim)
            query = q_buf[here, at]
            scores = dot(query, k_buf[before, at], ((1,), (1,)))
            scores = jnp.where(row >= col, scores, 0.0).astype(jnp.bfloat16)
            mixed = dot(scores, v_buf[before, at]) + dot(query, starts[b, i])
            level = lax.rsqrt(jnp.mean(mixed * mixed, axis=-1, keepdims=True) + 1e-06)
            att[here, at] = (mixed * level * og_ref[i]).astype(jnp.bfloat16)

    for bb in range(per_span):
        for r in range(0, BLOCK, step_rows):
            attend(1 - half, bb, r)
            first = (bb * BLOCK + r) // rows_here
            for head in range(first, first + step_rows // rows_here):
                send(att.at[slot(1 - half, head), :], out_ref.at[:, out_cols],
                     oz_send.at[head], oz_recv.at[h], {"ctx": partner, "head": head})
    for bb in range(per_span):
        for r in range(0, BLOCK, step_rows):
            attend(half, bb, r)
    for dh in range(1, n_head):
        send(att.at[slot(half, (h + dh) % n_head), :], out_ref.at[:, out_cols],
             o_send.at[dh], o_recv.at[dh], {"head": (h + dh) % n_head})
    own_out = pltpu.make_async_copy(att.at[slot(half, h), :], out_ref.at[:, out_cols], o_own)
    own_out.start()

    def out_place(head, side):
        return out_ref.at[:, pl.ds(pl.multiple_of((head * 2 + side) * width, width), width)]

    for head in range(n_head):
        arrived(out_place(head, 1 - half), oz_send.at[head], oz_recv.at[head])
    for dh in range(1, n_head):
        arrived(out_place((h + n_head - dh) % n_head, half), o_send.at[dh], o_recv.at[dh])
    own_out.wait()
    for copy in sent:
        copy.wait_send()


def on_device(n_ctx, n_head, tokens, in_gain, projections, prior_state, out_gain):
    rows_here, features = tokens.shape
    heads_here, dim, _ = prior_state.shape
    mine = heads_here // 2
    width = mine * dim
    n_tok = 2 * n_head * rows_here
    n_blocks = n_tok // BLOCK
    n_x = n_head // CORES
    cuts = min(4, projections.shape[1] // 32)
    dma = pltpu.SemaphoreType.DMA
    vmem = pl.BlockSpec(memory_space=pltpu.VMEM)
    bf16, f32 = jnp.bfloat16, jnp.float32
    return pl.pallas_call(
        functools.partial(kernel, n_ctx, n_head),
        out_shape=jax.ShapeDtypeStruct((rows_here, features), bf16),
        in_specs=[pl.BlockSpec(memory_space=pltpu.HBM)] * 5,
        out_specs=vmem,
        scratch_shapes=[
            pltpu.VMEM((rows_here, features), bf16),
            pltpu.VMEM((1, features), f32),
            pltpu.VMEM((mine, dim, dim), f32),
            pltpu.VMEM((mine, 1, dim), f32),
            dma((4,)),
            pltpu.VMEM((n_tok, features), bf16),
            pltpu.VMEM((3, features, width), bf16),
            pltpu.VMEM((n_tok, width), bf16),
            pltpu.VMEM((n_tok, width), bf16),
            pltpu.VMEM((n_tok, width), bf16),
            pltpu.VMEM((n_tok, width), bf16),
            pltpu.VMEM((n_blocks, mine, dim, dim), f32),
            pltpu.VMEM((mine, dim, dim), f32),
            pltpu.VMEM((n_ctx // 2, mine, dim, dim), f32),
            pltpu.VMEM((n_blocks, mine, dim, dim), bf16),
            dma, dma, dma,
            dma((n_x, 2)), dma((n_x, 2)), dma((n_x, 2)), dma((n_x, 2)),
            dma((3 * cuts, n_ctx)), dma((3 * cuts, n_ctx)),
            dma((3 * cuts, n_ctx)), dma((3 * cuts, n_ctx)),
            dma((n_ctx // 2,)), dma((n_ctx // 2,)),
            dma((n_head,)), dma((n_head,)), dma((n_head,)), dma((n_head,)), dma,
        ],
        compiler_params=pltpu.CompilerParams(
            collective_id=0, has_side_effects=True, vmem_limit_bytes=60 * 1024 * 1024
        ),
    )(
        tokens,
        in_gain.reshape(1, features),
        projections,
        prior_state,
        out_gain.reshape(heads_here, 1, dim),
    )


def solution(mesh):
    in_specs = (
        P(("runs", "ctx", "head"), None),
        P(),
        P(None, "ctx", "head"),
        P(("runs", "head"), None, None),
        P("head"),
    )
    out_specs = P(("runs", "ctx", "head"), None)
    return jax.shard_map(
        functools.partial(on_device, mesh.shape["ctx"], mesh.shape["head"]),
        mesh=mesh, in_specs=in_specs, out_specs=out_specs, check_vma=False,
    )
```

time: 74.6 us -> 66.5 us (0.89)
  Pallas kernels: 68.8 us -> 64.4 us
  local copies, waits for them, and re-layouts: 5.57 us -> 1.88 us
    pallas_call x1, Pallas kernels: 68.8 us -> 64.4 us  [on_device(): pl.pallas_call(functools.partial(kernel, n_ctx, n_head), out_shape=jax.Sh...]
    unnamed x11 -> x1, local copies, waits for them, and re-layouts: 5.57 us -> 1.88 us
where the time goes in v2:
time: 66.5 us; the launch traced here: 66.3 us
  Pallas kernels  64.4 us (97%)
  local copies, waits for them, and re-layouts  1.88 us (3%)
    pallas_call x1, Pallas kernels, on_device(): pl.pallas_call(functools.partial(kernel, n_ctx, n_head), out_shape=jax.Sh...  64.4 us
    unnamed x1, local copies, waits for them, and re-layouts  1.88 us

profile of v2, /device:TPU:0, one launch (start us, length us, event | category | flops | bytes accessed | tf_op | source)
XLA Modules:
  0.0 66.3 jit_solution(81971395327301868)
XLA Ops:
  0.0 64.4 %shard_map.55 = bf16[128,2048]{1,0:T(8,128)(2,1)} custom-call(bf16[128,2048]{1,0:T(8,128)(2,1)} %tok_hbm.1, f32[1,2048]{1,0:T(1,128)} %bitcast.2, bf16[3,512,512]{2,1,0:T(8,128)(2,1)} %w_ref.1, f32[4,128,128]{2,1,0:T(8,128)} %prior_hbm.1, f32[4,1,128]{2,1,0:T(1,128)} %bitcast.3), custom_call_target="tpu_custom_call" | custom-call | tf_op jit(solution)/shard_map/pallas_call | solution.py:294
  64.4 1.9 %copy.7 = bf16[128,2048]{1,0:T(8,128)(2,1)} copy(bf16[128,2048]{1,0:T(8,128)(2,1)} %shard_map.55) | data formatting | bytes 1048576

commit v3 on v2

--- a/solution.py
+++ b/solution.py
@@ -12,7 +12,7 @@
 MESH = pl.DeviceIdType.MESH
 QUERY, KEY, VALUE = 0, 1, 2
 AHEAD = 6
-AT_PARTNER, AT_FIRST, AT_SECOND, AT_KEYS, AT_VALUES = 2, 3, 7, 11, 12
+AT_PARTNER, AT_FIRST, AT_SECOND, AT_KEYS, AT_VALUES = 2, 3, 9, 10, 11
 
 
 def dot(a, b, contract=((1,), (0,))):
@@ -228,7 +228,6 @@
         work()
     do_starts()
     wait_weights(QUERY)
-    project(QUERY, q_buf)
 
     step_rows = 256
     out_cols = pl.ds(pl.multiple_of((h * 2 + half) * width, width), width)
@@ -240,6 +239,7 @@
         seen = r + step_rows
         here = pl.ds(pl.multiple_of(base + r, step_rows), step_rows)
         before = pl.ds(base, seen)
+        q_buf[here, :] = dot(x_buf[here, :], w_buf[QUERY]).astype(jnp.bfloat16)
         row = lax.broadcasted_iota(jnp.int32, (step_rows, seen), 0) + r
         col = lax.broadcasted_iota(jnp.int32, (step_rows, seen), 1)
         for i in range(mine):

time: 66.5 us -> 65.8 us (0.989)
  Pallas kernels: 64.4 us -> 63.7 us
    pallas_call x1, Pallas kernels: 64.4 us -> 63.7 us  [on_device(): pl.pallas_call(functools.partial(kernel, n_ctx, n_head), out_shape=jax.Sh...]
where the time goes in v3:
time: 65.8 us; the launch traced here: 65.6 us
  Pallas kernels  63.7 us (97%)
  local copies, waits for them, and re-layouts  1.88 us (3%)
    pallas_call x1, Pallas kernels, on_device(): pl.pallas_call(functools.partial(kernel, n_ctx, n_head), out_shape=jax.Sh...  63.7 us
    unnamed x1, local copies, waits for them, and re-layouts  1.88 us

profile of v3, /device:TPU:0, one launch (start us, length us, event | category | flops | bytes accessed | tf_op | source)
XLA Modules:
  0.0 65.6 jit_solution(6214445679280686633)
XLA Ops:
  0.0 63.7 %shard_map.55 = bf16[128,2048]{1,0:T(8,128)(2,1)} custom-call(bf16[128,2048]{1,0:T(8,128)(2,1)} %tok_hbm.1, f32[1,2048]{1,0:T(1,128)} %bitcast.2, bf16[3,512,512]{2,1,0:T(8,128)(2,1)} %w_ref.1, f32[4,128,128]{2,1,0:T(8,128)} %prior_hbm.1, f32[4,1,128]{2,1,0:T(1,128)} %bitcast.3), custom_call_target="tpu_custom_call" | custom-call | tf_op jit(solution)/shard_map/pallas_call | solution.py:294
  63.7 1.9 %copy.7 = bf16[128,2048]{1,0:T(8,128)(2,1)} copy(bf16[128,2048]{1,0:T(8,128)(2,1)} %shard_map.55) | data formatting | bytes 1048576

commit v4 on v3

--- a/solution.py
+++ b/solution.py
@@ -228,6 +228,7 @@
         work()
     do_starts()
     wait_weights(QUERY)
+    project(QUERY, q_buf)
 
     step_rows = 256
     out_cols = pl.ds(pl.multiple_of((h * 2 + half) * width, width), width)
@@ -239,7 +240,6 @@
         seen = r + step_rows
         here = pl.ds(pl.multiple_of(base + r, step_rows), step_rows)
         before = pl.ds(base, seen)
-        q_buf[here, :] = dot(x_buf[here, :], w_buf[QUERY]).astype(jnp.bfloat16)
         row = lax.broadcasted_iota(jnp.int32, (step_rows, seen), 0) + r
         col = lax.broadcasted_iota(jnp.int32, (step_rows, seen), 1)
         for i in range(mine):

time: 65.8 us -> 64.9 us (0.986)
  Pallas kernels: 63.7 us -> 62.7 us
    pallas_call x1, Pallas kernels: 63.7 us -> 62.7 us  [on_device(): pl.pallas_call(functools.partial(kernel, n_ctx, n_head), out_shape=jax.Sh...]
where the time goes in v4:
time: 64.9 us; the launch traced here: 64.6 us
  Pallas kernels  62.7 us (97%)
  local copies, waits for them, and re-layouts  1.88 us (3%)
    pallas_call x1, Pallas kernels, on_device(): pl.pallas_call(functools.partial(kernel, n_ctx, n_head), out_shape=jax.Sh...  62.7 us
    unnamed x1, local copies, waits for them, and re-layouts  1.88 us

profile of v4, /device:TPU:0, one launch (start us, length us, event | category | flops | bytes accessed | tf_op | source)
XLA Modules:
  0.0 64.6 jit_solution(6362855262907445239)
XLA Ops:
  0.0 62.7 %shard_map.55 = bf16[128,2048]{1,0:T(8,128)(2,1)} custom-call(bf16[128,2048]{1,0:T(8,128)(2,1)} %tok_hbm.1, f32[1,2048]{1,0:T(1,128)} %bitcast.2, bf16[3,512,512]{2,1,0:T(8,128)(2,1)} %w_ref.1, f32[4,128,128]{2,1,0:T(8,128)} %prior_hbm.1, f32[4,1,128]{2,1,0:T(1,128)} %bitcast.3), custom_call_target="tpu_custom_call" | custom-call | tf_op jit(solution)/shard_map/pallas_call | solution.py:294
  62.7 1.9 %copy.7 = bf16[128,2048]{1,0:T(8,128)(2,1)} copy(bf16[128,2048]{1,0:T(8,128)(2,1)} %shard_map.55) | data formatting | bytes 1048576
